TPU v7x, 128 devices: a whole 4x4x4 slice. The times are simulated.
128 devices in a mesh: dp: 32 (over z, x, core), mp: 4 (over y).
Axes of the slice: x: 4, y: 4, z: 4, core: 2. Of those that a mesh axis runs over, the one named last changes fastest.
Arguments:
- hidden: bfloat16 [40960, 8192], P('dp', 'mp'), may hold values from -6 to 6
- rewards: float32 [256, 160], P('dp'), may hold values from -4 to 4
- lengths: int32 [256], P('dp'), may hold values from 1 to 160, as said below
- dest_shard: int32 [256], P('dp'), may hold values from 0 to 31, as said below
- source_owner: int32 [256], P('dp'), may hold values from 0 to 31, as said below
- pack_offset: int32 [256], P('dp'), may hold values from 0 to 639, as said below
- segment_ids: int32 [20480], P('dp'), may hold values from 0 to 7, as said below
- norm_gain: float32 [8192], replicated, may hold values from 0.5 to 1.5
- w_query: bfloat16 [8192, 4096], P(None, 'mp'), may hold values from -1 to 1
- w_key: bfloat16 [8192, 512], P(None, 'mp'), may hold values from -1 to 1
- w_value: bfloat16 [8192, 512], P(None, 'mp'), may hold values from -0.0625 to 0.0625
- value_head: float32 [8192], P('mp'), may hold values from -0.0625 to 0.0625
- folded_head: float32 [4096], P('mp'), may hold values from -0.09375 to 0.09375
Outputs:
- values: float32 [256, 160], P('dp')
- advantages: float32 [256, 160], P('dp')
Inputs may be any that keep to these rules, and one draw needn't show every extreme that they name: `lengths`: rows of a slot past its rollout's length are unused. Every critic shard holds a rollout of 160 rows. Some owner's 8 rollouts all have 160 rows. `dest_shard`: owner o packs its 8 rollouts on the shards o, o + 1, ..., o + 7, modulo the number of shards, one on each. `source_owner`: shard s packs one rollout from each of the owners s, s - 1, ..., s - 7, modulo the number of shards, in some order, agreeing with dest_shard. `pack_offset`: A shard's packed rollouts lie back to back in the order of their index, each with the length that lengths gives it, and fill all 640 rows. `segment_ids`: each packed row names the index of the packed rollout that holds it, as pack_offset and lengths lay them out.
All inputs are finite; a program needn't handle non-finite values.
Results may differ from a plain program's by a relative error of at most 0.007.
Values may be sent and summed in bfloat16 or wider, within the bound.
A program may use at most 192 MiB of HBM per device.

v0:
```python
import math
import jax
import jax.numpy as jnp
from jax import lax
from jax.sharding import PartitionSpec as P

HD = 128
EPSILON = 1e-05
DISCOUNT = 0.99
SMOOTHING = 0.95
ROPE_BASE = 500000.0


def passed_along(value, axis, by):
    length = lax.axis_size(axis)
    return lax.ppermute(value, axis, [(i, (i + by) % length) for i in range(length)])


def rotary(values_in, positions):
    half_width = values_in.shape[-1] // 2
    frequency = ROPE_BASE ** (-jnp.arange(half_width, dtype=jnp.float32) / half_width)
    angles = positions.astype(jnp.float32)[:, None] * frequency[None, :]
    cosine = jnp.cos(angles)[:, None, :]
    sine_part = jnp.sin(angles)[:, None, :]
    front_half = values_in[..., :half_width]
    back_half = values_in[..., half_width:]
    return jnp.concatenate(
        [front_half * cosine - back_half * sine_part, back_half * cosine + front_half * sine_part],
        axis=-1,
    )


def head_values(queries, keys_out, values_out, segments, positions, folded_head):
    row_count = queries.shape[0]
    kv_count = keys_out.shape[1] // HD
    group_size = queries.shape[1] // HD // kv_count
    query_rot = rotary(queries.reshape(row_count, kv_count * group_size, HD), positions).astype(
        jnp.bfloat16
    )
    query_rot = query_rot.reshape(row_count, kv_count, group_size, HD)
    key_rot = rotary(keys_out.reshape(row_count, kv_count, HD), positions).astype(jnp.bfloat16)
    value_rows = values_out.astype(jnp.bfloat16).reshape(row_count, kv_count, HD)
    scores = jnp.einsum(
        "qhgd,khd->hgqk", query_rot, key_rot, preferred_element_type=jnp.float32
    ) / math.sqrt(HD)
    allowed = (segments[:, None] == segments[None, :]) & (positions[:, None] >= positions[None, :])
    scores = jnp.where(allowed[None, None], scores, -1e30)
    row_max = jnp.max(scores, axis=-1, keepdims=True)
    exp_scores = jnp.where(allowed[None, None], jnp.exp(scores - row_max), 0.0)
    row_total = jnp.sum(exp_scores, axis=-1, keepdims=True)
    weights = (exp_scores / row_total).astype(jnp.bfloat16)
    attended = jnp.einsum("hgqk,khd->qhgd", weights, value_rows, preferred_element_type=jnp.float32)
    return jnp.sum(attended.reshape(row_count, -1) * folded_head[None, :], axis=1)


def local(
    hidden,
    rewards,
    lengths,
    dest_shard,
    source_owner,
    pack_offset,
    segment_ids,
    norm_gain,
    w_query,
    w_key,
    w_value,
    value_head,
    folded_head,
):
    shards = lax.axis_size("dp")
    shard_index = lax.axis_index("dp")
    rollouts = lengths.shape[0]
    slot_rows = rewards.shape[1]
    packed_rows = segment_ids.shape[0]
    part_width = hidden.shape[1]
    slot_lanes = jnp.arange(rollouts, dtype=jnp.int32)

    def slot_for(shift_by):
        target = (shard_index + shift_by) % shards
        return jnp.sum(jnp.where(dest_shard == target, slot_lanes, 0))

    def outgoing(shift_by, source):
        return lax.dynamic_slice_in_dim(source, slot_for(shift_by) * slot_rows, slot_rows, 0)

    source_step = (shard_index - source_owner) % shards
    lane_match = segment_ids[:, None] == slot_lanes[None, :]
    row_step = jnp.sum(jnp.where(lane_match, source_step[None, :], 0), axis=1)
    row_offset = jnp.sum(jnp.where(lane_match, pack_offset[None, :], 0), axis=1)
    positions = jnp.arange(packed_rows, dtype=jnp.int32) - row_offset
    pick_rows = row_step * slot_rows + positions
    full_rows = lax.all_gather(hidden, "mp", axis=1, tiled=True)
    received = [outgoing(0, full_rows)]
    for shift_by in range(1, rollouts):
        received.append(passed_along(outgoing(shift_by, full_rows), "dp", shift_by))
    packed = jnp.take(jnp.concatenate(received, axis=0), pick_rows, axis=0)
    packed_f = packed.astype(jnp.float32)
    row_scale = lax.rsqrt(jnp.mean(packed_f * packed_f, axis=1) + EPSILON)
    normed = (packed_f * row_scale[:, None] * norm_gain[None, :]).astype(jnp.bfloat16)
    queries = jnp.dot(normed, w_query, preferred_element_type=jnp.float32)
    keys_out = jnp.dot(normed, w_key, preferred_element_type=jnp.float32)
    values_out = jnp.dot(normed, w_value, preferred_element_type=jnp.float32)
    own_part = lax.dynamic_slice_in_dim(packed, lax.axis_index("mp") * part_width, part_width, 1)
    value_terms = head_values(queries, keys_out, values_out, segment_ids, positions, folded_head)
    value_terms = value_terms + jnp.sum(own_part.astype(jnp.float32) * value_head[None, :], axis=1)
    packed_values = lax.psum(value_terms, "mp")
    padded = jnp.concatenate([packed_values, jnp.zeros((slot_rows,), jnp.float32)])
    slot_values = jnp.zeros((rollouts, slot_rows), jnp.float32)
    for shift_by in range(rollouts):
        owner_now = (shard_index - shift_by) % shards
        j_index = jnp.sum(jnp.where(source_owner == owner_now, slot_lanes, 0))
        start_at = jnp.sum(jnp.where(slot_lanes == j_index, pack_offset, 0))
        arrived = lax.dynamic_slice_in_dim(padded, start_at, slot_rows, 0)
        if shift_by:
            arrived = passed_along(arrived, "dp", -shift_by)
        slot_values = jnp.where(
            (slot_lanes == slot_for(shift_by))[:, None], arrived[None, :], slot_values
        )
    step_ids = jnp.arange(slot_rows, dtype=jnp.int32)
    live_mask = step_ids[None, :] < lengths[:, None]
    values = jnp.where(live_mask, slot_values, 0.0)
    next_live = step_ids[None, :] + 1 < lengths[:, None]
    following = jnp.concatenate([values[:, 1:], jnp.zeros((rollouts, 1), jnp.float32)], axis=1)
    one_step = jnp.where(
        live_mask, rewards + DISCOUNT * jnp.where(next_live, following, 0.0) - values, 0.0
    )
    lag_matrix = (step_ids[:, None] - step_ids[None, :]).astype(jnp.float32)
    decay_table = jnp.where(
        lag_matrix >= 0, jnp.exp(lag_matrix * math.log(DISCOUNT * SMOOTHING)), 0.0
    )
    advantages = jnp.dot(one_step, decay_table, precision=lax.Precision.HIGHEST)
    return (values, advantages)


def solution(mesh):
    return jax.shard_map(
        local,
        mesh=mesh,
        in_specs=(
            P("dp", "mp"),
            P("dp", None),
            P("dp"),
            P("dp"),
            P("dp"),
            P("dp"),
            P("dp"),
            P(),
            P(None, "mp"),
            P(None, "mp"),
            P(None, "mp"),
            P("mp"),
            P("mp"),
        ),
        out_specs=(P("dp", None), P("dp", None)),
        check_vma=False,
    )
```

profile of v0, /device:TPU:1, one launch (start us, length us, event | category | flops | bytes accessed | tf_op | source)
XLA Modules:
  0.0 709.8 jit_solution(8402809665676939686)
XLA Ops:
  7.2 0.7 all-gather.2.cloned.1.call-update
  8.1 1.7 fusion.49
  15.0 187.3 %all-gather.2.cloned.1.call-done = bf16[1280,8192]{1,0:T(8,128)(2,1)} async-done(((bf16[1280,2048]{1,0:T(8,128)(2,1)}), bf16[1280,8192]{1,0:T(8,128)(2,1)}) %all-gather.2.cloned.1.call-update) | async-done | bytes 20971536 | tf_op jit(solution)/shard_map/all_gather | solution.py:92
  202.3 14.7 %constant_dynamic-slice_fusion = (bf16[160,8192]{1,0:T(8,128)(2,1)}, bf16[160,8192]{1,0:T(8,128)(2,1)}, bf16[160,8192]{1,0:T(8,128)(2,1)}, bf16[160,8192]{1,0:T(...) fusion(bf16[1280,8192]{1,0:T(8,128)(2,1)} %all-gather.2.cloned., ...), kind=kLoop, calls=%fused_computation.95 | loop fusion | bytes 41943072 | tf_op jit(solution)/shard_map/dynamic_slice | solution.py:84
  217.0 2.0 collective-permute-start
  219.0 5.7 fusion.58
  239.8 0.7 iota_compare_fusion.10
  240.5 1.3 collective-permute-start.1
  241.7 0.7 iota_compare_fusion.3
  243.0 0.7 iota_compare_fusion.5
  243.7 0.6 iota_compare_fusion.6
  244.4 0.7 iota_compare_fusion.7
  245.0 1.6 collective-permute-start.2
  247.0 1.2 multiply_cosine_fusion
  248.3 1.6 collective-permute-start.3
  249.9 3.0 collective-permute-start.4
  252.9 0.9 collective-permute-done
  253.8 2.5 collective-permute-start.5
  256.3 3.5 constant_dynamic-update-slice_fusion.6
  259.8 54.1 %collective-permute-done.1 = bf16[160,8192]{1,0:T(8,128)(2,1)S(1)} collective-permute-done((bf16[160,8192]{1,0:T(8,128)(2,1)}, bf16[160,8192]{1,0:T(8,128)(2,1)S(1)}, u32[]{:S(2)}, u32[]{:S(2)}) %collective-permute-start.1) | collective-permute-done | bytes 2621472 | tf_op jit(solution)/shard_map/ppermute | solution.py:16
  313.9 1.7 constant_dynamic-update-slice_fusion.5
  315.7 50.5 %collective-permute-done.2 = bf16[160,8192]{1,0:T(8,128)(2,1)S(1)} collective-permute-done((bf16[160,8192]{1,0:T(8,128)(2,1)}, bf16[160,8192]{1,0:T(8,128)(2,1)S(1)}, u32[]{:S(2)}, u32[]{:S(2)}) %collective-permute-start.2) | collective-permute-done | bytes 2621472 | tf_op jit(solution)/shard_map/ppermute | solution.py:16
  366.2 1.8 constant_dynamic-update-slice_fusion.4
  368.0 99.9 %collective-permute-done.3 = bf16[160,8192]{1,0:T(8,128)(2,1)S(1)} collective-permute-done((bf16[160,8192]{1,0:T(8,128)(2,1)}, bf16[160,8192]{1,0:T(8,128)(2,1)S(1)}, u32[]{:S(2)}, u32[]{:S(2)}) %collective-permute-start.3) | collective-permute-done | bytes 2621472 | tf_op jit(solution)/shard_map/ppermute | solution.py:16
  467.9 1.7 constant_dynamic-update-slice_fusion.3
  469.6 33.6 %collective-permute-done.4 = bf16[160,8192]{1,0:T(8,128)(2,1)S(1)} collective-permute-done((bf16[160,8192]{1,0:T(8,128)(2,1)}, bf16[160,8192]{1,0:T(8,128)(2,1)S(1)}, u32[]{:S(2)}, u32[]{:S(2)}) %collective-permute-start.4) | collective-permute-done | bytes 2621472 | tf_op jit(solution)/shard_map/ppermute | solution.py:16
  503.2 1.7 constant_dynamic-update-slice_fusion.2
  504.9 51.4 %collective-permute-done.5 = bf16[160,8192]{1,0:T(8,128)(2,1)S(1)} collective-permute-done((bf16[160,8192]{1,0:T(8,128)(2,1)}, bf16[160,8192]{1,0:T(8,128)(2,1)S(1)}, u32[]{:S(2)}, u32[]{:S(2)}) %collective-permute-start.5) | collective-permute-done | bytes 2621472 | tf_op jit(solution)/shard_map/ppermute | solution.py:16
  556.3 1.7 constant_dynamic-update-slice_fusion.1
  558.0 29.1 %collective-permute-done.6 = bf16[160,8192]{1,0:T(8,128)(2,1)S(1)} collective-permute-done((bf16[160,8192]{1,0:T(8,128)(2,1)}, bf16[160,8192]{1,0:T(8,128)(2,1)S(1)}, u32[]{:S(2)}, u32[]{:S(2)}) %collective-permute-start.6) | collective-permute-done | bytes 2621472 | tf_op jit(solution)/shard_map/ppermute | solution.py:16
  587.2 1.7 constant_dynamic-update-slice_fusion
  588.8 31.5 %gather_fusion = bf16[640,8192]{1,0:T(8,128)(2,1)} fusion(bf16[1280,8192]{1,0:T(8,128)(2,1)} %constant_dynamic-update-slice_fusion, s32[1024]{0:T(1024)S(1)} %pad_clamp_fusion), kind=kCustom, calls=%fused_computation | custom fusion | bytes 20974080 | tf_op jit(solution)/shard_map/jit(_take)/gather | solution.py:96
  620.3 7.7 %fusion = (f32[640]{0:T(1024)S(1)}, bf16[640,8192]{1,0:T(8,128)(2,1)S(1)}) fusion(bf16[640,8192]{1,0:T(8,128)(2,1)} %gather_fusion, pred[640]{0:T(1024)(128)(4,1)S(1)} %compare_and_fusion.1), kind=kLoop, calls=%fused_computation.3 | loop fusion | flops 20970880 | bytes 20974720 | tf_op jit(solution)/shard_map/reduce_sum | solution.py:98
  628.0 3.3 convolution_bitcast_fusion.1
  631.3 0.7 fusion.36
  632.0 14.4 %convolution_bitcast_fusion = f32[80,8,8,128]{3,1,2,0:T(8,128)S(1)} fusion(bf16[8192,1024]{1,0:T(8,128)(2,1)} %param.21, bf16[640,8192]{1,0:T(8,128)(2,1)S(1)} %get-tuple-element.29, f32[8192]{0:T(1024)S(1)} %copy-done.8, f32[640]{0:T(1024)S(1)} %add_rsqrt_fusion), kind=kOutput, calls=%fused_computation.20 | convolution fusion | flops 10758389760 | bytes 29919744 | tf_op jit(solution)/shard_map/dot_general | solution.py:100
  647.0 0.8 fusion.86
  647.9 1.0 subtract_convert_fusion
  648.9 6.4 fusion.3
  655.3 7.8 %fusion.4 = f32[8,640]{1,0:T(8,128)S(1)} fusion(f32[640,640,8]{1,0,2:T(8,128)} %get-tuple-element.58, f32[8,640]{1,0:T(8,128)S(1)} %get-tuple-element.57, pred[640,640]{0,1:T(8,128)(4,1)S(1)} %compare_and_fusion), kind=kLoop, calls=%fused_computation.11 | loop fusion | flops 16378880 | bytes 13557760 | tf_op jit(solution)/shard_map/reduce_sum | solution.py:50
  663.8 14.8 %fusion.7 = f32[640]{0:T(1024)S(1)} fusion(f32[8,640]{1,0:T(8,128)S(1)} %fusion.4, f32[8,640]{1,0:T(8,128)S(1)} %get-tuple-element.57, f32[640,640,8]{1,0,2:T(8,128)} %get-tuple-element.58, pred[640,640]{0,1:T(8,128)(4,1)S(1)} %compare_and_fusion, f32[8,128]{1,0:T(8,128)S(1)} %bitcast.51, bf16[8192,128]{1,0:T(8,128)(2,1)} %param.23, ...), kind=kOutput, calls=%fused_computation.16 | convolution fusion | flops 2223062528 | bytes 26182656 | tf_op jit(solution)/shard_map/hgqk,khd->qhgd/dot_general | solution.py:52
  678.6 6.7 psum.7
  685.6 0.6 iota_compare_fusion.8
  686.2 9.0 %collective-permute-start.12 = (f32[160]{0:T(256)S(1)}, f32[160]{0:T(256)S(1)}, u32[]{:S(2)}, u32[]{:S(2)}) collective-permute-start(f32[160]{0:T(256)S(1)} %get-tuple-element.51), channel_id=1, source_target_pairs={{0,120},{4,124},{8,0},{12,4},{16,8},{20,12},{24,16},{28,20},{32,24... | collective-permute-start | bytes 1928 | tf_op jit(solution)/shard_map/ppermute | solution.py:16
  695.2 1.9 collective-permute-start.7
  698.4 2.4 collective-permute-done.8
  700.8 0.9 collective-permute-done.9
  701.9 0.8 fusion.25
  (52 shorter events, 4.0 us)
Async XLA Ops:
  7.2 620.9 %copy-start = (bf16[8192,128]{1,0:T(8,128)(2,1)S(1)}, bf16[8192,128]{1,0:T(8,128)(2,1)}, u32[]{:S(2)}) copy-start(bf16[8192,128]{1,0:T(8,128)(2,1)} %param.22) | copy-start | bytes 6291460
  7.2 195.1 %all-gather.2.cloned.1.call-start = ((), (), s32[]{:S(2)}) async-start(), calls=%async_computation | async-start | bytes 26214400 | tf_op jit(solution)/shard_map/all_gather | solution.py:92
  14.9 204.1 %copy-start.6 = (s32[8]{0:T(128)S(1)}, s32[8]{0:T(128)}, u32[]{:S(2)}) copy-start(s32[8]{0:T(128)} %param.18) | copy-start | bytes 100
  15.0 224.7 %copy-start.3 = (s32[640]{0:T(1024)S(1)}, s32[640]{0:T(1024)}, u32[]{:S(2)}) copy-start(s32[640]{0:T(1024)} %param.19) | copy-start | bytes 7684
  217.0 36.8 %collective-permute-start = (bf16[160,8192]{1,0:T(8,128)(2,1)}, bf16[160,8192]{1,0:T(8,128)(2,1)}, u32[]{:S(2)}, u32[]{:S(2)}) collective-permute-start(bf16[160,8192]{1,0:T(8,128)(2,1)} %get-tuple-element.36), channel_id=1, source_target_pairs={{0,4},{4,8},{8,12},{12,16},{16,20},{20,24},{24,28},{28,32},{32,36}... | collective-permute-start | bytes 7864328 | tf_op jit(solution)/shard_map/ppermute | solution.py:16
  240.5 73.5 %collective-permute-start.1 = (bf16[160,8192]{1,0:T(8,128)(2,1)}, bf16[160,8192]{1,0:T(8,128)(2,1)S(1)}, u32[]{:S(2)}, u32[]{:S(2)}) collective-permute-start(bf16[160,8192]{1,0:T(8,128)(2,1)} %get-tuple-element.35), channel_id=1, source_target_pairs={{0,8},{4,12},{8,16},{12,20},{16,24},{20,28},{24,32},{28,36},{32,40... | collective-permute-start | bytes 7864328 | tf_op jit(solution)/shard_map/ppermute | solution.py:16
  245.0 121.1 %collective-permute-start.2 = (bf16[160,8192]{1,0:T(8,128)(2,1)}, bf16[160,8192]{1,0:T(8,128)(2,1)S(1)}, u32[]{:S(2)}, u32[]{:S(2)}) collective-permute-start(bf16[160,8192]{1,0:T(8,128)(2,1)} %get-tuple-element.34), channel_id=1, source_target_pairs={{0,12},{4,16},{8,20},{12,24},{16,28},{20,32},{24,36},{28,40},{32,4... | collective-permute-start | bytes 7864328 | tf_op jit(solution)/shard_map/ppermute | solution.py:16
  248.3 219.6 %collective-permute-start.3 = (bf16[160,8192]{1,0:T(8,128)(2,1)}, bf16[160,8192]{1,0:T(8,128)(2,1)S(1)}, u32[]{:S(2)}, u32[]{:S(2)}) collective-permute-start(bf16[160,8192]{1,0:T(8,128)(2,1)} %get-tuple-element.33), channel_id=1, source_target_pairs={{0,16},{4,20},{8,24},{12,28},{16,32},{20,36},{24,40},{28,44},{32,4... | collective-permute-start | bytes 7864328 | tf_op jit(solution)/shard_map/ppermute | solution.py:16
  249.9 253.3 %collective-permute-start.4 = (bf16[160,8192]{1,0:T(8,128)(2,1)}, bf16[160,8192]{1,0:T(8,128)(2,1)S(1)}, u32[]{:S(2)}, u32[]{:S(2)}) collective-permute-start(bf16[160,8192]{1,0:T(8,128)(2,1)} %get-tuple-element.32), channel_id=1, source_target_pairs={{0,20},{4,24},{8,28},{12,32},{16,36},{20,40},{24,44},{28,48},{32,5... | collective-permute-start | bytes 7864328 | tf_op jit(solution)/shard_map/ppermute | solution.py:16
  253.8 302.5 %collective-permute-start.5 = (bf16[160,8192]{1,0:T(8,128)(2,1)}, bf16[160,8192]{1,0:T(8,128)(2,1)S(1)}, u32[]{:S(2)}, u32[]{:S(2)}) collective-permute-start(bf16[160,8192]{1,0:T(8,128)(2,1)} %get-tuple-element.31), channel_id=1, source_target_pairs={{0,24},{4,28},{8,32},{12,36},{16,40},{20,44},{24,48},{28,52},{32,5... | collective-permute-start | bytes 7864328 | tf_op jit(solution)/shard_map/ppermute | solution.py:16
  313.9 273.2 %collective-permute-start.6 = (bf16[160,8192]{1,0:T(8,128)(2,1)}, bf16[160,8192]{1,0:T(8,128)(2,1)S(1)}, u32[]{:S(2)}, u32[]{:S(2)}) collective-permute-start(bf16[160,8192]{1,0:T(8,128)(2,1)} %get-tuple-element.30), channel_id=1, source_target_pairs={{0,28},{4,32},{8,36},{12,40},{16,44},{20,48},{24,52},{28,56},{32,6... | collective-permute-start | bytes 7864328 | tf_op jit(solution)/shard_map/ppermute | solution.py:16
  620.3 7.7 %copy-start.8 = (f32[8192]{0:T(1024)S(1)}, f32[8192]{0:T(1024)}, u32[]{:S(2)}) copy-start(f32[8192]{0:T(1024)} %param.20) | copy-start | bytes 98308
  628.0 35.1 %copy-start.2 = (bf16[640,8192]{1,0:T(8,128)(2,1)}, bf16[640,8192]{1,0:T(8,128)(2,1)S(1)}, u32[]{:S(2)}) copy-start(bf16[640,8192]{1,0:T(8,128)(2,1)S(1)} %get-tuple-element.29) | copy-start | bytes 31457284
  655.3 7.9 %copy-start.5 = (f32[2048]{0:T(1024)S(1)}, f32[2048]{0:T(1024)}, u32[]{:S(2)}) copy-start(f32[2048]{0:T(1024)} %param.24) | copy-start | bytes 24580
  655.3 8.5 %copy-start.10 = (f32[1024]{0:T(1024)S(1)}, f32[1024]{0:T(1024)}, u32[]{:S(2)}) copy-start(f32[1024]{0:T(1024)} %param.25) | copy-start | bytes 12292
  663.8 37.9 %copy-start.7 = (s32[8]{0:T(128)S(1)}, s32[8]{0:T(128)}, u32[]{:S(2)}) copy-start(s32[8]{0:T(128)} %param.15) | copy-start | bytes 100
  663.8 38.1 %copy-start.9 = (f32[8,160]{1,0:T(8,128)S(1)}, f32[8,160]{1,0:T(8,128)}, u32[]{:S(2)}) copy-start(f32[8,160]{1,0:T(8,128)} %param.14) | copy-start | bytes 15364
  663.8 38.9 %copy-start.1 = (bf16[8192,128]{1,0:T(8,128)(2,1)S(1)}, bf16[8192,128]{1,0:T(8,128)(2,1)}, u32[]{:S(2)}) copy-start(bf16[8192,128]{1,0:T(8,128)(2,1)} %param.22) | copy-start | bytes 6291460
  685.5 11.7 %collective-permute-start.10 = (f32[160]{0:T(256)S(1)}, f32[160]{0:T(256)S(1)}, u32[]{:S(2)}, u32[]{:S(2)}) collective-permute-start(f32[160]{0:T(256)S(1)} %get-tuple-element.49), channel_id=1, source_target_pairs={{0,112},{4,116},{8,120},{12,124},{16,0},{20,4},{24,8},{28,12},{32,... | collective-permute-start | bytes 1928 | tf_op jit(solution)/shard_map/ppermute | solution.py:16
  685.5 11.7 %collective-permute-start.11 = (f32[160]{0:T(256)S(1)}, f32[160]{0:T(256)S(1)}, u32[]{:S(2)}, u32[]{:S(2)}) collective-permute-start(f32[160]{0:T(256)S(1)} %get-tuple-element.50), channel_id=1, source_target_pairs={{0,116},{4,120},{8,124},{12,0},{16,4},{20,8},{24,12},{28,16},{32,2... | collective-permute-start | bytes 1928 | tf_op jit(solution)/shard_map/ppermute | solution.py:16
  686.2 12.1 %collective-permute-start.12 = (f32[160]{0:T(256)S(1)}, f32[160]{0:T(256)S(1)}, u32[]{:S(2)}, u32[]{:S(2)}) collective-permute-start(f32[160]{0:T(256)S(1)} %get-tuple-element.51), channel_id=1, source_target_pairs={{0,120},{4,124},{8,0},{12,4},{16,8},{20,12},{24,16},{28,20},{32,24... | collective-permute-start | bytes 1928 | tf_op jit(solution)/shard_map/ppermute | solution.py:16
  695.2 3.1 collective-permute-start.13
  695.2 3.1 collective-permute-start.7
  697.2 3.6 collective-permute-start.8
  697.2 4.5 collective-permute-start.9
  701.8 0.9 copy-start.4
Sparse Core Ops, SparseCore 0:
  9.7 192.5 all-gather.1
where the time goes:
time: 718 us; the launch traced here: 710 us
  waiting for transfers between devices  511 us (71%)
  local copies, waits for them, and re-layouts  61.7 us (9%)
  matrix products  39.7 us (6%)
  between operations  34.9 us (5%)
  other arithmetic  32.1 us (4%)
  starting transfers between devices  23.6 us (3%)
    ppermute x14, waiting for transfers between devices, passed_along(): lax.ppermute(value, axis, [(i, (i + by) % length) for i in range(length)])  323 us
    all_gather x1, waiting for transfers between devices, local(): full_rows = lax.all_gather(hidden, 'mp', axis=1, tiled=True)  187 us
    gather x1, local copies, waits for them, and re-layouts, local(): packed = jnp.take(jnp.concatenate(received, axis=0), pick_rows, axis=0)  31.5 us
    ppermute x14, starting transfers between devices, passed_along(): lax.ppermute(value, axis, [(i, (i + by) % length) for i in range(length)])  23.6 us
    dot_general x1, matrix products, head_values(): jnp.einsum('hgqk,khd->qhgd', weights, value_rows, preferred_element_type=...  14.8 us
    dynamic_slice x1, local copies, waits for them, and re-layouts, outgoing(): lax.dynamic_slice_in_dim(source, slot_for(shift_by) * slot_rows, slot_row...  14.7 us
    dot_general x1, matrix products, local(): queries = jnp.dot(normed, w_query, preferred_element_type=jnp.float32)  14.4 us
  transfers between devices with their start and end apart: 15, of which 10 were waited for; matrix products, arithmetic and copies ran while one was open for 4% of the time, Pallas kernels for 0%

commit v1 on v0

--- a/solution.py
+++ b/solution.py
@@ -89,7 +89,9 @@
     row_offset = jnp.sum(jnp.where(lane_match, pack_offset[None, :], 0), axis=1)
     positions = jnp.arange(packed_rows, dtype=jnp.int32) - row_offset
     pick_rows = row_step * slot_rows + positions
-    full_rows = lax.all_gather(hidden, "mp", axis=1, tiled=True)
+    full_rows = jnp.concatenate(
+        lax.all_to_all(jnp.stack([hidden] * lax.axis_size("mp")), "mp", 0, 0), axis=1
+    )
     received = [outgoing(0, full_rows)]
     for shift_by in range(1, rollouts):
         received.append(passed_along(outgoing(shift_by, full_rows), "dp", shift_by))

time: 718 us -> 775 us (1.079)
  waiting for transfers between devices: 511 us -> 545 us
  local copies, waits for them, and re-layouts: 61.7 us -> 88.5 us
  between operations: 34.9 us -> 21.5 us
  starting transfers between devices: 23.6 us -> 33.3 us
    all_to_all x0 -> x1, waiting for transfers between devices: none -> 223 us  [local(): lax.all_to_all(jnp.stack([hidden] * lax.axis_size('mp')), 'mp', 0, 0)]
    all_gather x1 -> x0, waiting for transfers between devices: 187 us -> none  [local(): full_rows = lax.all_gather(hidden, 'mp', axis=1, tiled=True)]
    reshape x0 -> x1, local copies, waits for them, and re-layouts: none -> 17.5 us  [local(): jnp.concatenate(lax.all_to_all(jnp.stack([hidden] * lax.axis_size('mp')),...]
    another operation x0 -> x1, local copies, waits for them, and re-layouts: none -> 9.25 us  [local(): jnp.stack([hidden] * lax.axis_size('mp'))]
    all_to_all x0 -> x1, starting transfers between devices: none -> 7.84 us  [local(): lax.all_to_all(jnp.stack([hidden] * lax.axis_size('mp')), 'mp', 0, 0)]
  transfers between devices with their start and end apart: 15 -> 15, of which waited for: 10 -> 11; matrix products, arithmetic and copies ran while one was open for 4% -> 3% of each run, Pallas kernels for 0% -> 0%
where the time goes in v1:
time: 775 us; the launch traced here: 766 us
  waiting for transfers between devices  545 us (70%)
  local copies, waits for them, and re-layouts  88.5 us (11%)
  matrix products  39.7 us (5%)
  starting transfers between devices  33.3 us (4%)
  other arithmetic  31.4 us (4%)
  between operations  21.5 us (3%)
    ppermute x14, waiting for transfers between devices, passed_along(): lax.ppermute(value, axis, [(i, (i + by) % length) for i in range(length)])  322 us
    all_to_all x1, waiting for transfers between devices, local(): lax.all_to_all(jnp.stack([hidden] * lax.axis_size('mp')), 'mp', 0, 0)  223 us
    gather x1, local copies, waits for them, and re-layouts, local(): packed = jnp.take(jnp.concatenate(received, axis=0), pick_rows, axis=0)  31.5 us
    ppermute x14, starting transfers between devices, passed_along(): lax.ppermute(value, axis, [(i, (i + by) % length) for i in range(length)])  25.4 us
    reshape x1, local copies, waits for them, and re-layouts, local(): jnp.concatenate(lax.all_to_all(jnp.stack([hidden] * lax.axis_size('mp')),...  17.5 us
  transfers between devices with their start and end apart: 15, of which 11 were waited for; matrix products, arithmetic and copies ran while one was open for 3% of the time, Pallas kernels for 0%

profile of v1, /device:TPU:1, one launch (start us, length us, event | category | flops | bytes accessed | tf_op | source)
XLA Modules:
  0.0 766.4 jit_solution(4902990976845659869)
XLA Ops:
  0.6 9.2 %stack.2 = bf16[4,1280,2048]{2,1,0:T(8,128)(2,1)} broadcast(bf16[1280,2048]{1,0:T(8,128)(2,1)} %param.13), dimensions={1,2} | broadcast | bytes 26214400 | tf_op jit(solution)/shard_map/stack | solution.py:93
  9.9 7.8 %all-to-all-start = ((bf16[4,1280,2048]{2,1,0:T(8,128)(2,1)}), bf16[4,1280,2048]{2,1,0:T(8,128)(2,1)}, u32[]{:S(2)}, u32[]{:S(2)}) async-start(bf16[4,1280,2048]{2,1,0:T(8,128)(2,1)} %stack.2), calls=%async_computation | async-start | bytes 41943040 | tf_op jit(solution)/shard_map/all_to_all | solution.py:93
  18.0 1.0 fusion.49
  24.1 222.7 %all-to-all-done = bf16[4,1280,2048]{2,1,0:T(8,128)(2,1)} async-done(((bf16[4,1280,2048]{2,1,0:T(8,128)(2,1)}), bf16[4,1280,2048]{2,1,0:T(8,128)(2,1)}, u32[]{:S(2)}, u32[]{:S(2)}) %all-to-all-start) | async-done | bytes 20971552 | tf_op jit(solution)/shard_map/all_to_all | solution.py:93
  246.8 17.5 %copy.42 = bf16[4,160,8,2048]{3,2,0,1:T(8,128)(2,1)} copy(bf16[4,160,8,2048]{3,2,1,0:T(8,128)(2,1)} %bitcast.14) | data formatting | bytes 41943040 | tf_op jit(solution)/shard_map/reshape | solution.py:92
  264.3 14.7 %constant_dynamic-slice_fusion = (bf16[160,8192]{1,0:T(8,128)(2,1)}, bf16[160,8192]{1,0:T(8,128)(2,1)}, bf16[160,8192]{1,0:T(8,128)(2,1)}, bf16[160,8192]{1,0:T(...) fusion(bf16[1280,8192]{1,0:T(8,128)(2,1)} %bitcast.53, ...), kind=kLoop, calls=%fused_computation.95 | loop fusion | bytes 41943072 | tf_op jit(solution)/shard_map/dynamic_slice | solution.py:84
  279.0 2.6 collective-permute-start
  281.6 5.7 fusion.58
  302.4 0.7 iota_compare_fusion.10
  303.1 1.3 collective-permute-start.1
  304.4 0.7 iota_compare_fusion.3
  305.6 0.7 iota_compare_fusion.5
  306.3 0.6 iota_compare_fusion.6
  307.0 0.7 iota_compare_fusion.7
  307.7 1.6 collective-permute-start.2
  309.7 1.2 multiply_cosine_fusion
  310.9 1.9 collective-permute-start.3
  312.8 3.4 collective-permute-start.4
  316.4 2.8 collective-permute-start.5
  319.3 3.5 constant_dynamic-update-slice_fusion.6
  322.8 52.9 %collective-permute-done.1 = bf16[160,8192]{1,0:T(8,128)(2,1)S(1)} collective-permute-done((bf16[160,8192]{1,0:T(8,128)(2,1)}, bf16[160,8192]{1,0:T(8,128)(2,1)S(1)}, u32[]{:S(2)}, u32[]{:S(2)}) %collective-permute-start.1) | collective-permute-done | bytes 2621472 | tf_op jit(solution)/shard_map/ppermute | solution.py:16
  375.6 1.7 constant_dynamic-update-slice_fusion.5
  377.4 51.4 %collective-permute-done.2 = bf16[160,8192]{1,0:T(8,128)(2,1)S(1)} collective-permute-done((bf16[160,8192]{1,0:T(8,128)(2,1)}, bf16[160,8192]{1,0:T(8,128)(2,1)S(1)}, u32[]{:S(2)}, u32[]{:S(2)}) %collective-permute-start.2) | collective-permute-done | bytes 2621472 | tf_op jit(solution)/shard_map/ppermute | solution.py:16
  428.8 1.8 constant_dynamic-update-slice_fusion.4
  430.6 101.0 %collective-permute-done.3 = bf16[160,8192]{1,0:T(8,128)(2,1)S(1)} collective-permute-done((bf16[160,8192]{1,0:T(8,128)(2,1)}, bf16[160,8192]{1,0:T(8,128)(2,1)S(1)}, u32[]{:S(2)}, u32[]{:S(2)}) %collective-permute-start.3) | collective-permute-done | bytes 2621472 | tf_op jit(solution)/shard_map/ppermute | solution.py:16
  531.6 1.7 constant_dynamic-update-slice_fusion.3
  533.3 33.6 %collective-permute-done.4 = bf16[160,8192]{1,0:T(8,128)(2,1)S(1)} collective-permute-done((bf16[160,8192]{1,0:T(8,128)(2,1)}, bf16[160,8192]{1,0:T(8,128)(2,1)S(1)}, u32[]{:S(2)}, u32[]{:S(2)}) %collective-permute-start.4) | collective-permute-done | bytes 2621472 | tf_op jit(solution)/shard_map/ppermute | solution.py:16
  566.9 1.7 constant_dynamic-update-slice_fusion.2
  568.6 53.1 %collective-permute-done.5 = bf16[160,8192]{1,0:T(8,128)(2,1)S(1)} collective-permute-done((bf16[160,8192]{1,0:T(8,128)(2,1)}, bf16[160,8192]{1,0:T(8,128)(2,1)S(1)}, u32[]{:S(2)}, u32[]{:S(2)}) %collective-permute-start.5) | collective-permute-done | bytes 2621472 | tf_op jit(solution)/shard_map/ppermute | solution.py:16
  621.7 1.7 constant_dynamic-update-slice_fusion.1
  623.4 26.7 %collective-permute-done.6 = bf16[160,8192]{1,0:T(8,128)(2,1)S(1)} collective-permute-done((bf16[160,8192]{1,0:T(8,128)(2,1)}, bf16[160,8192]{1,0:T(8,128)(2,1)S(1)}, u32[]{:S(2)}, u32[]{:S(2)}) %collective-permute-start.6) | collective-permute-done | bytes 2621472 | tf_op jit(solution)/shard_map/ppermute | solution.py:16
  650.1 1.7 constant_dynamic-update-slice_fusion
  651.8 31.5 %gather_fusion = bf16[640,8192]{1,0:T(8,128)(2,1)} fusion(bf16[1280,8192]{1,0:T(8,128)(2,1)} %constant_dynamic-update-slice_fusion, s32[1024]{0:T(1024)S(1)} %pad_clamp_fusion), kind=kCustom, calls=%fused_computation | custom fusion | bytes 20974080 | tf_op jit(solution)/shard_map/jit(_take)/gather | solution.py:98
  683.3 7.7 %fusion = (f32[640]{0:T(1024)S(1)}, bf16[640,8192]{1,0:T(8,128)(2,1)S(1)}) fusion(bf16[640,8192]{1,0:T(8,128)(2,1)} %gather_fusion, pred[640]{0:T(1024)(128)(4,1)S(1)} %compare_and_fusion.1), kind=kLoop, calls=%fused_computation.3 | loop fusion | flops 20970880 | bytes 20974720 | tf_op jit(solution)/shard_map/reduce_sum | solution.py:100
  691.0 3.3 convolution_bitcast_fusion.1
  694.3 0.7 fusion.36
  695.0 14.4 %convolution_bitcast_fusion = f32[80,8,8,128]{3,1,2,0:T(8,128)S(1)} fusion(bf16[8192,1024]{1,0:T(8,128)(2,1)} %param.21, bf16[640,8192]{1,0:T(8,128)(2,1)S(1)} %get-tuple-element.29, f32[8192]{0:T(1024)S(1)} %copy-done.10, f32[640]{0:T(1024)S(1)} %add_rsqrt_fusion), kind=kOutput, calls=%fused_computation.20 | convolution fusion | flops 10758389760 | bytes 29919744 | tf_op jit(solution)/shard_map/dot_general | solution.py:102
  710.0 0.8 fusion.86
  710.8 1.0 subtract_convert_fusion
  711.8 6.4 fusion.3
  718.2 7.8 %fusion.4 = f32[8,640]{1,0:T(8,128)S(1)} fusion(f32[640,640,8]{1,0,2:T(8,128)} %get-tuple-element.58, f32[8,640]{1,0:T(8,128)S(1)} %get-tuple-element.57, pred[640,640]{0,1:T(8,128)(4,1)S(1)} %compare_and_fusion), kind=kLoop, calls=%fused_computation.11 | loop fusion | flops 16378880 | bytes 13557760 | tf_op jit(solution)/shard_map/reduce_sum | solution.py:50
  726.7 14.8 %fusion.7 = f32[640]{0:T(1024)S(1)} fusion(f32[8,640]{1,0:T(8,128)S(1)} %fusion.4, f32[8,640]{1,0:T(8,128)S(1)} %get-tuple-element.57, f32[640,640,8]{1,0,2:T(8,128)} %get-tuple-element.58, pred[640,640]{0,1:T(8,128)(4,1)S(1)} %compare_and_fusion, f32[8,128]{1,0:T(8,128)S(1)} %bitcast.55, bf16[8192,128]{1,0:T(8,128)(2,1)} %param.23, ...), kind=kOutput, calls=%fused_computation.16 | convolution fusion | flops 2223062528 | bytes 26182656 | tf_op jit(solution)/shard_map/hgqk,khd->qhgd/dot_general | solution.py:52
  741.6 6.9 psum.7
  749.3 9.7 %collective-permute-start.12 = (f32[160]{0:T(256)S(1)}, f32[160]{0:T(256)S(1)}, u32[]{:S(2)}, u32[]{:S(2)}) collective-permute-start(f32[160]{0:T(256)S(1)} %get-tuple-element.51), channel_id=1, source_target_pairs={{0,120},{4,124},{8,0},{12,4},{16,8},{20,12},{24,16},{28,20},{32,24... | collective-permute-start | bytes 1928 | tf_op jit(solution)/shard_map/ppermute | solution.py:16
  759.1 1.6 collective-permute-start.7
  762.1 2.2 collective-permute-done.8
  764.3 0.9 collective-permute-done.9
  765.3 0.8 fusion.25
  (57 shorter events, 5.0 us)
Async XLA Ops:
  0.6 690.3 %copy-start = (bf16[8192,128]{1,0:T(8,128)(2,1)S(1)}, bf16[8192,128]{1,0:T(8,128)(2,1)}, u32[]{:S(2)}) copy-start(bf16[8192,128]{1,0:T(8,128)(2,1)} %param.22) | copy-start | bytes 6291460
  9.9 8.1 %copy-start.7 = (s32[8]{0:T(128)S(1)}, s32[8]{0:T(128)}, u32[]{:S(2)}) copy-start(s32[8]{0:T(128)} %param.16) | copy-start | bytes 100
  9.9 8.1 %copy-start.8 = (s32[8]{0:T(128)S(1)}, s32[8]{0:T(128)}, u32[]{:S(2)}) copy-start(s32[8]{0:T(128)} %param.17) | copy-start | bytes 100
  9.9 236.8 %all-to-all-start = ((bf16[4,1280,2048]{2,1,0:T(8,128)(2,1)}), bf16[4,1280,2048]{2,1,0:T(8,128)(2,1)}, u32[]{:S(2)}, u32[]{:S(2)}) async-start(bf16[4,1280,2048]{2,1,0:T(8,128)(2,1)} %stack.2), calls=%async_computation | async-start | bytes 41943040 | tf_op jit(solution)/shard_map/all_to_all | solution.py:93
  264.3 17.3 %copy-start.6 = (s32[8]{0:T(128)S(1)}, s32[8]{0:T(128)}, u32[]{:S(2)}) copy-start(s32[8]{0:T(128)} %param.18) | copy-start | bytes 100
  264.3 38.0 %copy-start.3 = (s32[640]{0:T(1024)S(1)}, s32[640]{0:T(1024)}, u32[]{:S(2)}) copy-start(s32[640]{0:T(1024)} %param.19) | copy-start | bytes 7684
  279.0 37.4 %collective-permute-start = (bf16[160,8192]{1,0:T(8,128)(2,1)}, bf16[160,8192]{1,0:T(8,128)(2,1)}, u32[]{:S(2)}, u32[]{:S(2)}) collective-permute-start(bf16[160,8192]{1,0:T(8,128)(2,1)} %get-tuple-element.36), channel_id=1, source_target_pairs={{0,4},{4,8},{8,12},{12,16},{16,20},{20,24},{24,28},{28,32},{32,36}... | collective-permute-start | bytes 7864328 | tf_op jit(solution)/shard_map/ppermute | solution.py:16
  303.1 72.6 %collective-permute-start.1 = (bf16[160,8192]{1,0:T(8,128)(2,1)}, bf16[160,8192]{1,0:T(8,128)(2,1)S(1)}, u32[]{:S(2)}, u32[]{:S(2)}) collective-permute-start(bf16[160,8192]{1,0:T(8,128)(2,1)} %get-tuple-element.35), channel_id=1, source_target_pairs={{0,8},{4,12},{8,16},{12,20},{16,24},{20,28},{24,32},{28,36},{32,40... | collective-permute-start | bytes 7864328 | tf_op jit(solution)/shard_map/ppermute | solution.py:16
  307.7 121.1 %collective-permute-start.2 = (bf16[160,8192]{1,0:T(8,128)(2,1)}, bf16[160,8192]{1,0:T(8,128)(2,1)S(1)}, u32[]{:S(2)}, u32[]{:S(2)}) collective-permute-start(bf16[160,8192]{1,0:T(8,128)(2,1)} %get-tuple-element.34), channel_id=1, source_target_pairs={{0,12},{4,16},{8,20},{12,24},{16,28},{20,32},{24,36},{28,40},{32,4... | collective-permute-start | bytes 7864328 | tf_op jit(solution)/shard_map/ppermute | solution.py:16
  310.9 220.7 %collective-permute-start.3 = (bf16[160,8192]{1,0:T(8,128)(2,1)}, bf16[160,8192]{1,0:T(8,128)(2,1)S(1)}, u32[]{:S(2)}, u32[]{:S(2)}) collective-permute-start(bf16[160,8192]{1,0:T(8,128)(2,1)} %get-tuple-element.33), channel_id=1, source_target_pairs={{0,16},{4,20},{8,24},{12,28},{16,32},{20,36},{24,40},{28,44},{32,4... | collective-permute-start | bytes 7864328 | tf_op jit(solution)/shard_map/ppermute | solution.py:16
  312.8 254.1 %collective-permute-start.4 = (bf16[160,8192]{1,0:T(8,128)(2,1)}, bf16[160,8192]{1,0:T(8,128)(2,1)S(1)}, u32[]{:S(2)}, u32[]{:S(2)}) collective-permute-start(bf16[160,8192]{1,0:T(8,128)(2,1)} %get-tuple-element.32), channel_id=1, source_target_pairs={{0,20},{4,24},{8,28},{12,32},{16,36},{20,40},{24,44},{28,48},{32,5... | collective-permute-start | bytes 7864328 | tf_op jit(solution)/shard_map/ppermute | solution.py:16
  316.4 305.3 %collective-permute-start.5 = (bf16[160,8192]{1,0:T(8,128)(2,1)}, bf16[160,8192]{1,0:T(8,128)(2,1)S(1)}, u32[]{:S(2)}, u32[]{:S(2)}) collective-permute-start(bf16[160,8192]{1,0:T(8,128)(2,1)} %get-tuple-element.31), channel_id=1, source_target_pairs={{0,24},{4,28},{8,32},{12,36},{16,40},{20,44},{24,48},{28,52},{32,5... | collective-permute-start | bytes 7864328 | tf_op jit(solution)/shard_map/ppermute | solution.py:16
  375.6 274.5 %collective-permute-start.6 = (bf16[160,8192]{1,0:T(8,128)(2,1)}, bf16[160,8192]{1,0:T(8,128)(2,1)S(1)}, u32[]{:S(2)}, u32[]{:S(2)}) collective-permute-start(bf16[160,8192]{1,0:T(8,128)(2,1)} %get-tuple-element.30), channel_id=1, source_target_pairs={{0,28},{4,32},{8,36},{12,40},{16,44},{20,48},{24,52},{28,56},{32,6... | collective-permute-start | bytes 7864328 | tf_op jit(solution)/shard_map/ppermute | solution.py:16
  683.3 7.7 %copy-start.10 = (f32[8192]{0:T(1024)S(1)}, f32[8192]{0:T(1024)}, u32[]{:S(2)}) copy-start(f32[8192]{0:T(1024)} %param.20) | copy-start | bytes 98308
  691.0 35.1 %copy-start.2 = (bf16[640,8192]{1,0:T(8,128)(2,1)}, bf16[640,8192]{1,0:T(8,128)(2,1)S(1)}, u32[]{:S(2)}) copy-start(bf16[640,8192]{1,0:T(8,128)(2,1)S(1)} %get-tuple-element.29) | copy-start | bytes 31457284
  718.2 7.9 %copy-start.5 = (f32[2048]{0:T(1024)S(1)}, f32[2048]{0:T(1024)}, u32[]{:S(2)}) copy-start(f32[2048]{0:T(1024)} %param.24) | copy-start | bytes 24580
  718.2 8.5 %copy-start.12 = (f32[1024]{0:T(1024)S(1)}, f32[1024]{0:T(1024)}, u32[]{:S(2)}) copy-start(f32[1024]{0:T(1024)} %param.25) | copy-start | bytes 12292
  726.7 38.4 %copy-start.9 = (s32[8]{0:T(128)S(1)}, s32[8]{0:T(128)}, u32[]{:S(2)}) copy-start(s32[8]{0:T(128)} %param.15) | copy-start | bytes 100
  726.7 38.6 %copy-start.11 = (f32[8,160]{1,0:T(8,128)S(1)}, f32[8,160]{1,0:T(8,128)}, u32[]{:S(2)}) copy-start(f32[8,160]{1,0:T(8,128)} %param.14) | copy-start | bytes 15364
  726.7 39.4 %copy-start.1 = (bf16[8192,128]{1,0:T(8,128)(2,1)S(1)}, bf16[8192,128]{1,0:T(8,128)(2,1)}, u32[]{:S(2)}) copy-start(bf16[8192,128]{1,0:T(8,128)(2,1)} %param.22) | copy-start | bytes 6291460
  748.6 12.1 %collective-permute-start.10 = (f32[160]{0:T(256)S(1)}, f32[160]{0:T(256)S(1)}, u32[]{:S(2)}, u32[]{:S(2)}) collective-permute-start(f32[160]{0:T(256)S(1)} %get-tuple-element.49), channel_id=1, source_target_pairs={{0,112},{4,116},{8,120},{12,124},{16,0},{20,4},{24,8},{28,12},{32,... | collective-permute-start | bytes 1928 | tf_op jit(solution)/shard_map/ppermute | solution.py:16
  748.6 12.0 %collective-permute-start.11 = (f32[160]{0:T(256)S(1)}, f32[160]{0:T(256)S(1)}, u32[]{:S(2)}, u32[]{:S(2)}) collective-permute-start(f32[160]{0:T(256)S(1)} %get-tuple-element.50), channel_id=1, source_target_pairs={{0,116},{4,120},{8,124},{12,0},{16,4},{20,8},{24,12},{28,16},{32,2... | collective-permute-start | bytes 1928 | tf_op jit(solution)/shard_map/ppermute | solution.py:16
  749.3 12.3 %collective-permute-start.12 = (f32[160]{0:T(256)S(1)}, f32[160]{0:T(256)S(1)}, u32[]{:S(2)}, u32[]{:S(2)}) collective-permute-start(f32[160]{0:T(256)S(1)} %get-tuple-element.51), channel_id=1, source_target_pairs={{0,120},{4,124},{8,0},{12,4},{16,8},{20,12},{24,16},{28,20},{32,24... | collective-permute-start | bytes 1928 | tf_op jit(solution)/shard_map/ppermute | solution.py:16
  759.1 3.0 collective-permute-start.13
  759.1 3.0 collective-permute-start.7
  760.6 3.6 collective-permute-start.8
  760.6 4.5 collective-permute-start.9
  765.2 0.9 copy-start.4
